TPU v7x, 256 devices: a whole 4x4x8 slice. The times are simulated.
256 devices in a mesh: ctx: 32 (over x, z), grp: 8 (over y, core).
Axes of the slice: x: 4, y: 4, z: 8, core: 2. Of those that a mesh axis runs over, the one named last changes fastest.
Arguments:
- out_grad: bfloat16 [16384, 2048], P('ctx', 'grp'), may hold values from -6 to 6
- filter_mats: bfloat16 [16, 2048, 2048], P('grp', 'ctx'), may hold values from -0.125 to 0.125
- coeffs: float32 [16, 80], replicated, may hold values from -0.15625 to 0.15625
- pole_rates: float32 [80], replicated, may hold values from 1.2207031e-06 to 0.03
Outputs:
- in_grad: bfloat16 [16384, 2048], P('ctx', 'grp')
All inputs are finite; a program needn't handle non-finite values.
Results may differ from a plain program's by a relative error of at most 0.001.
Values may be sent and summed in bfloat16 or wider, within the bound.
A program may use at most 128 MiB of HBM per device.

v0:
```python
import jax
import jax.numpy as jnp
from jax import lax
from jax.sharding import PartitionSpec as P

exact_prec = lax.Precision.HIGHEST


def entering(array, axis, combine, identity):
    count, here = (lax.axis_size(axis), lax.axis_index(axis))
    everything = jax.tree.map(lambda part: lax.all_gather(part, axis), array)
    start = jax.tree.map(
        lambda part, zero: jnp.broadcast_to(jnp.asarray(zero, part.dtype), part.shape),
        array,
        identity,
    )

    def step(k, before):
        at = count - 1 - k
        reached = at > here
        new = combine(before, jax.tree.map(lambda part: part[at], everything))
        return jax.tree.map(lambda a, b: jnp.where(reached, a, b), new, before)

    return lax.fori_loop(0, count, step, start)


def merge_suffix(earlier, latter):
    carried_e, factor_e = earlier
    carried_l, factor_l = latter
    return (carried_l + factor_l * carried_e, factor_l * factor_e)


def per_device(out_grad, filter_mats, coeffs, pole_rates):
    full_grad = lax.all_gather(out_grad, "grp", axis=1, tiled=True)
    length = full_grad.shape[0]
    col_width = out_grad.shape[1]
    poles = pole_rates.shape[0]
    positions = jnp.arange(length, dtype=jnp.float32)
    pole_gains = jnp.sqrt(-jnp.expm1(-2.0 * pole_rates))
    middle = float(length // 2)
    rising = jnp.exp(-(positions[:, None] - middle) * pole_rates[None, :])
    falling = jnp.exp((positions[:, None] - middle) * pole_rates[None, :])
    causal = positions[:, None] >= positions[None, :]
    decay_pos = jnp.exp(-positions[:, None] * pole_rates[None, :])
    edge_decay = pole_gains[None, :] * jnp.exp(-(length - positions)[:, None] * pole_rates[None, :])
    block_decay = jnp.exp(-length * pole_rates)[:, None]
    unit_factor = jnp.ones((poles, 1), jnp.float32)
    filters = filter_mats.shape[0]
    own_coeffs = lax.dynamic_slice_in_dim(coeffs, lax.axis_index("grp") * filters, filters, 0)
    kernel_mat = jnp.einsum(
        "tp,kp,sp->kts", rising, own_coeffs * pole_gains[None, :], falling, precision=exact_prec
    )
    kernel_mat = jnp.where(causal[None], kernel_mat, 0.0)
    weights = own_coeffs[:, :, None] * decay_pos.T[None]
    proj_grad = jnp.einsum(
        "tj,kij->kti",
        full_grad,
        lax.all_gather(filter_mats, "ctx", axis=1, tiled=True),
        preferred_element_type=jnp.float32,
    )
    near_part = jnp.einsum("kts,kti->si", kernel_mat, proj_grad, precision=exact_prec)
    pole_part = jnp.einsum("kpt,kti->pi", weights, proj_grad, precision=exact_prec)
    stacked = jnp.concatenate([near_part, pole_part], axis=0)
    near_sum = lax.psum_scatter(stacked[:length], "grp", scatter_dimension=1, tiled=True)
    pole_sum = lax.psum(stacked[length:], "grp")
    later_all = entering(
        (pole_sum, block_decay), "ctx", merge_suffix, (jnp.zeros_like(pole_sum), unit_factor)
    )[0]
    own_cols = lax.dynamic_slice_in_dim(later_all, lax.axis_index("grp") * col_width, col_width, 1)
    total = near_sum + jnp.dot(edge_decay, own_cols, precision=exact_prec)
    return total.astype(jnp.bfloat16)


def solution(mesh):
    placed = (P("ctx", "grp"), P("grp", "ctx", None), P(), P())
    return jax.shard_map(
        per_device, mesh=mesh, in_specs=placed, out_specs=P("ctx", "grp"), check_vma=False
    )
```

profile of v0, /device:TPU:0, one launch (start us, length us, event | category | flops | bytes accessed | tf_op | source)
XLA Modules:
  0.0 490.5 jit_solution(5679977234924721466)
XLA Ops:
  8.1 1.3 dynamic-slice
  12.2 27.7 %all-gather.7.cloned.1.call-done = bf16[512,2048]{1,0:T(8,128)(2,1)} async-done(((bf16[512,256]{1,0:T(8,128)(2,1)}), bf16[512,2048]{1,0:T(8,128)(2,1)}) %all-gather.7.cloned.1.call-update) | async-done | bytes 2097168 | tf_op jit(solution)/shard_map/all_gather | solution.py:34
  39.9 143.1 %all-gather.5.cloned.1.call-done = bf16[2,2048,2048]{2,1,0:T(8,128)(2,1)} async-done(((bf16[2,64,2048]{2,1,0:T(8,128)(2,1)}), bf16[2,2048,2048]{2,1,0:T(8,128)(2,1)}) %all-gather.5.cloned.1.call-update) | async-done | bytes 16777232 | tf_op jit(solution)/shard_map/all_gather | solution.py:58
  183.0 12.9 %fusion.11 = f32[2,2048,512]{2,1,0:T(8,128)S(1)} fusion(bf16[2,2048,2048]{2,1,0:T(8,128)(2,1)} %all-gather.5.cloned.1.call-done, bf16[512,2048]{1,0:T(8,128)(2,1)} %all-gather.7.cloned.1.call-done), kind=kOutput, calls=%fused_computation.9 | convolution fusion | flops 8589934592 | bytes 27262976 | tf_op jit(solution)/shard_map/tj,kij->kti/dot_general | solution.py:55
  195.9 3.3 copy-done
  199.2 9.1 %fusion.8 = f32[1,80,2048]{2,1,0:T(8,128)} fusion(f32[2,2048,512]{2,1,0:T(8,128)S(1)} %fusion.11, f32[80,512]{1,0:T(8,128)S(1)} %multiply_exponential_fusion, f32[2,80]{1,0:T(2,128)S(1)} %get-tuple-element.167), kind=kOutput, calls=%fused_computation.8 | convolution fusion | flops 2013347840 | bytes 9208448 | tf_op jit(solution)/shard_map/kpt,kti->pi/dot_general | solution.py:62
  208.3 63.9 %all-reduce.3.cloned.1.call-done = f32[1,80,2048]{2,1,0:T(8,128)} async-done(((f32[1,80,2048]{2,1,0:T(8,128)}), f32[1,80,2048]{2,1,0:T(8,128)}) %all-reduce.3.cloned.1.call-update) | async-done | bytes 655376 | tf_op jit(solution)/shard_map/psum | solution.py:65
  272.4 147.7 %all-reduce = f32[2560]{0:T(1024)S(1)} all-reduce(f32[2560]{0:T(1024)S(1)} %get-tuple-element.168), channel_id=2, replica_groups=mesh['ctx'=32,'grp'=8] {'ctx'}, use_global_device_ids=true, to_apply=%add | all-reduce | flops 2560 | bytes 20480
  420.7 1.9 fusion.17
  422.6 17.5 %fusion.5 = f32[512,2048]{1,0:T(8,128)} fusion(f32[2,2048,512]{2,1,0:T(8,128)} %copy-done, f32[2,512,512]{1,2,0:T(8,128)S(1)} %fusion.17, pred[512,512]{0,1:T(8,128)(4,1)S(1)} %iota_compare_fusion), kind=kOutput, calls=%fused_computation.7 | convolution fusion | flops 12885426176 | bytes 14942208 | tf_op jit(solution)/shard_map/kts,kti->si/dot_general | solution.py:61
  440.1 41.4 %while.16 = (s32[]{:T(128)}, f32[80,2048]{1,0:T(8,128)S(1)}, s32[]{:T(128)}, f32[32,80,2048]{2,1,0:T(8,128)}, f32[32,80,1]{1,2,0:T(1,128)S(1)}, /*index=5*/s32[]{:T(128)}, s32[]{:T(128)}, s32[]{:T(128)}, s32[]{:T(128)}) while((s32[]{:T(128)}, f32[80,2048]{1,0:T(8,128)S(1)}, s32[]{:T(128)}, f32[32,80,2048]{2,1,0:T(8,128)}, ...), condition=%wide.region_3.4_spmd.clone, body=%wide.region_2.3_spmd.clone.sunk | while | flops 655368 | bytes 1967215 | solution.py:24
  446.6 1.3 fusion.39
  450.5 1.2 fusion.39
  451.8 1.3 fusion.39
  453.1 1.2 fusion.39
  454.4 1.2 fusion.39
  455.7 1.2 fusion.39
  459.6 1.2 fusion.39
  462.1 1.3 fusion.39
  466.0 1.3 fusion.39
  467.3 1.3 fusion.39
  468.6 1.2 fusion.39
  469.9 1.2 fusion.39
  481.5 2.5 fusion.14
  (81 shorter events, 29.6 us)
Async XLA Ops:
  6.5 33.4 %all-gather.7.cloned.1.call-start = ((), (), s32[]{:S(2)}) async-start(), calls=%async_computation.2 | async-start | bytes 2359296 | tf_op jit(solution)/shard_map/all_gather | solution.py:34
  7.3 175.8 %all-gather.5.cloned.1.call-start = ((), (), s32[]{:S(2)}) async-start(), calls=%async_computation.1 | async-start | bytes 17301504 | tf_op jit(solution)/shard_map/all_gather | solution.py:58
  8.0 264.2 %all-reduce.3.cloned.1.call-start = ((), (), s32[]{:S(2)}) async-start(), calls=%async_computation.4 | async-start | bytes 1310720 | tf_op jit(solution)/shard_map/psum | solution.py:65
  195.9 3.3 copy-start
  195.9 224.5 %copy-start.1 = (f32[80]{0:T(128)S(1)}, f32[80]{0:T(128)}, u32[]{:S(2)}) copy-start(f32[80]{0:T(128)} %param.9) | copy-start | bytes 964
  208.3 231.8 %all-gather.9.cloned.1.call-start = ((), (), s32[]{:S(2)}) async-start(), calls=%async_computation.5 | async-start | bytes 21626880 | tf_op jit(solution)/shard_map/all_gather | solution.py:11
  272.2 209.3 %reduce-scatter.2.cloned.1.call-start = ((), (), s32[]{:S(2)}) async-start(), calls=%async_computation.3 | async-start | bytes 4718592 | tf_op jit(solution)/shard_map/reduce_scatter | solution.py:64
Sparse Core Ops, SparseCore 0:
  9.2 30.7 all-gather.6
  42.5 140.4 all-gather.4
  208.4 63.7 all-reduce.2
  274.6 161.0 all-gather.8
  440.2 35.2 reduce-scatter.1
where the time goes:
time: 492 us; the launch traced here: 491 us
  waiting for transfers between devices  236 us (48%)
  blocking collectives  148 us (30%)
  matrix products  43.8 us (9%)
  other arithmetic  42.5 us (9%)
  between operations  13.9 us (3%)
  local copies, waits for them, and re-layouts  4.96 us (1%)
    unnamed x1, blocking collectives  148 us
    all_gather x1, waiting for transfers between devices, per_device(): lax.all_gather(filter_mats, 'ctx', axis=1, tiled=True)  143 us
    psum x1, waiting for transfers between devices, per_device(): pole_sum = lax.psum(stacked[length:], 'grp')  63.9 us
    select_n x32, other arithmetic, step(): return jax.tree.map(lambda a, b: jnp.where(reached, a, b), new, before)  39.8 us
    all_gather x1, waiting for transfers between devices, per_device(): full_grad = lax.all_gather(out_grad, 'grp', axis=1, tiled=True)  27.7 us
    dot_general x1, matrix products, per_device(): jnp.einsum('kts,kti->si', kernel_mat, proj_grad, precision=exact_prec)  17.5 us
    dot_general x1, matrix products, per_device(): jnp.einsum('tj,kij->kti', full_grad, lax.all_gather(filter_mats, 'ctx', a...  12.9 us
  transfers between devices with their start and end apart: 5, of which 3 were waited for; matrix products, arithmetic and copies ran while one was open for 13% of the time, Pallas kernels for 0%

commit v1 on v0

--- a/solution.py
+++ b/solution.py
@@ -62,7 +62,7 @@
     pole_part = jnp.einsum("kpt,kti->pi", weights, proj_grad, precision=exact_prec)
     stacked = jnp.concatenate([near_part, pole_part], axis=0)
     near_sum = lax.psum_scatter(stacked[:length], "grp", scatter_dimension=1, tiled=True)
-    pole_sum = lax.psum(stacked[length:], "grp")
+    pole_sum = jnp.sum(lax.all_gather(stacked[length:], "grp"), axis=0)
     later_all = entering(
         (pole_sum, block_decay), "ctx", merge_suffix, (jnp.zeros_like(pole_sum), unit_factor)
     )[0]

time: 492 us -> 469 us (0.953)
  waiting for transfers between devices: 236 us -> 208 us
    psum x1 -> x0, waiting for transfers between devices: 63.9 us -> none  [per_device(): pole_sum = lax.psum(stacked[length:], 'grp')]
    all_gather x0 -> x1, waiting for transfers between devices: none -> 36.2 us  [per_device(): pole_sum = jnp.sum(lax.all_gather(stacked[length:], 'grp'), axis=0)]
  transfers between devices with their start and end apart: 5 -> 5, of which waited for: 3 -> 3; matrix products, arithmetic and copies ran while one was open for 13% -> 14% of each run, Pallas kernels for 0% -> 0%
where the time goes in v1:
time: 469 us; the launch traced here: 466 us
  waiting for transfers between devices  208 us (44%)
  blocking collectives  147 us (31%)
  other arithmetic  46.3 us (10%)
  matrix products  43.7 us (9%)
  between operations  13.9 us (3%)
  local copies, waits for them, and re-layouts  4.97 us (1%)
    unnamed x1, blocking collectives  147 us
    all_gather x1, waiting for transfers between devices, per_device(): lax.all_gather(filter_mats, 'ctx', axis=1, tiled=True)  143 us
    select_n x32, other arithmetic, step(): return jax.tree.map(lambda a, b: jnp.where(reached, a, b), new, before)  39.8 us
    all_gather x1, waiting for transfers between devices, per_device(): pole_sum = jnp.sum(lax.all_gather(stacked[length:], 'grp'), axis=0)  36.2 us
    all_gather x1, waiting for transfers between devices, per_device(): full_grad = lax.all_gather(out_grad, 'grp', axis=1, tiled=True)  27.7 us
    dot_general x1, matrix products, per_device(): jnp.einsum('kts,kti->si', kernel_mat, proj_grad, precision=exact_prec)  17.4 us
    dot_general x1, matrix products, per_device(): jnp.einsum('tj,kij->kti', full_grad, lax.all_gather(filter_mats, 'ctx', a...  12.9 us
  transfers between devices with their start and end apart: 5, of which 3 were waited for; matrix products, arithmetic and copies ran while one was open for 14% of the time, Pallas kernels for 0%

profile of v1, /device:TPU:0, one launch (start us, length us, event | category | flops | bytes accessed | tf_op | source)
XLA Modules:
  0.0 466.4 jit_solution(10913260917682523133)
XLA Ops:
  8.1 1.3 dynamic-slice
  12.2 27.7 %all-gather.10.cloned.1.call-done = bf16[512,2048]{1,0:T(8,128)(2,1)} async-done(((bf16[512,256]{1,0:T(8,128)(2,1)}), bf16[512,2048]{1,0:T(8,128)(2,1)}) %all-gather.10.cloned.1.call-update) | async-done | bytes 2097168 | tf_op jit(solution)/shard_map/all_gather | solution.py:34
  39.9 143.1 %all-gather.8.cloned.1.call-done = bf16[2,2048,2048]{2,1,0:T(8,128)(2,1)} async-done(((bf16[2,64,2048]{2,1,0:T(8,128)(2,1)}), bf16[2,2048,2048]{2,1,0:T(8,128)(2,1)}) %all-gather.8.cloned.1.call-update) | async-done | bytes 16777232 | tf_op jit(solution)/shard_map/all_gather | solution.py:58
  183.0 12.9 %fusion.11 = f32[2,2048,512]{2,1,0:T(8,128)S(1)} fusion(bf16[2,2048,2048]{2,1,0:T(8,128)(2,1)} %all-gather.8.cloned.1.call-done, bf16[512,2048]{1,0:T(8,128)(2,1)} %all-gather.10.cloned.1.call-done), kind=kOutput, calls=%fused_computation.9 | convolution fusion | flops 8589934592 | bytes 27262976 | tf_op jit(solution)/shard_map/tj,kij->kti/dot_general | solution.py:55
  195.9 3.3 copy-done
  199.2 9.1 %fusion.8 = f32[80,2048]{1,0:T(8,128)} fusion(f32[2,2048,512]{2,1,0:T(8,128)S(1)} %fusion.11, f32[80,512]{1,0:T(8,128)S(1)} %multiply_exponential_fusion, f32[2,80]{1,0:T(2,128)S(1)} %get-tuple-element.167), kind=kOutput, calls=%fused_computation.8 | convolution fusion | flops 2013347840 | bytes 9208448 | tf_op jit(solution)/shard_map/kpt,kti->pi/dot_general | solution.py:62
  208.3 36.2 %all-gather.12.cloned.1.call-done = f32[640,2048]{1,0:T(8,128)} async-done(((f32[80,2048]{1,0:T(8,128)}), f32[640,2048]{1,0:T(8,128)}) %all-gather.12.cloned.1.call-update) | async-done | bytes 5242896 | tf_op jit(solution)/shard_map/all_gather | solution.py:65
  244.6 3.7 reduce_sum.9
  248.5 147.5 %all-reduce = f32[2560]{0:T(1024)S(1)} all-reduce(f32[2560]{0:T(1024)S(1)} %get-tuple-element.168), channel_id=4, replica_groups=mesh['ctx'=32,'grp'=8] {'ctx'}, use_global_device_ids=true, to_apply=%add | all-reduce | flops 2560 | bytes 20480
  396.6 1.9 fusion.17
  398.5 17.4 %fusion.5 = f32[512,2048]{1,0:T(8,128)} fusion(f32[2,2048,512]{2,1,0:T(8,128)} %copy-done, f32[2,512,512]{1,2,0:T(8,128)S(1)} %fusion.17, pred[512,512]{0,1:T(8,128)(4,1)S(1)} %iota_compare_fusion), kind=kOutput, calls=%fused_computation.7 | convolution fusion | flops 12885426176 | bytes 14942208 | tf_op jit(solution)/shard_map/kts,kti->si/dot_general | solution.py:61
  416.0 41.4 %while.16 = (s32[]{:T(128)}, f32[80,2048]{1,0:T(8,128)S(1)}, s32[]{:T(128)}, f32[32,80,2048]{2,1,0:T(8,128)}, f32[32,80,1]{1,2,0:T(1,128)S(1)}, /*index=5*/s32[]{:T(128)}, s32[]{:T(128)}, s32[]{:T(128)}, s32[]{:T(128)}) while((s32[]{:T(128)}, f32[80,2048]{1,0:T(8,128)S(1)}, s32[]{:T(128)}, f32[32,80,2048]{2,1,0:T(8,128)}, ...), condition=%wide.region_3.4_spmd.clone, body=%wide.region_2.3_spmd.clone.sunk | while | flops 655368 | bytes 1967215 | solution.py:24
  421.2 1.3 fusion.39
  426.4 1.2 fusion.39
  427.7 1.2 fusion.39
  429.0 1.3 fusion.39
  430.3 1.3 fusion.39
  434.2 1.3 fusion.39
  435.5 1.3 fusion.39
  440.6 1.3 fusion.39
  441.9 1.2 fusion.39
  443.2 1.2 fusion.39
  444.5 1.3 fusion.39
  457.4 2.5 fusion.14
  (82 shorter events, 30.9 us)
Async XLA Ops:
  6.5 33.4 %all-gather.10.cloned.1.call-start = ((), (), s32[]{:S(2)}) async-start(), calls=%async_computation.2 | async-start | bytes 2359296 | tf_op jit(solution)/shard_map/all_gather | solution.py:34
  7.3 175.8 %all-gather.8.cloned.1.call-start = ((), (), s32[]{:S(2)}) async-start(), calls=%async_computation.1 | async-start | bytes 17301504 | tf_op jit(solution)/shard_map/all_gather | solution.py:58
  8.0 236.6 %all-gather.12.cloned.1.call-start = ((), (), s32[]{:S(2)}) async-start(), calls=%async_computation.4 | async-start | bytes 5898240 | tf_op jit(solution)/shard_map/all_gather | solution.py:65
  195.9 3.3 copy-start
  199.2 197.2 %copy-start.1 = (f32[80]{0:T(128)S(1)}, f32[80]{0:T(128)}, u32[]{:S(2)}) copy-start(f32[80]{0:T(128)} %param.9) | copy-start | bytes 964
  208.3 207.7 %all-gather.14.cloned.1.call-start = ((), (), s32[]{:S(2)}) async-start(), calls=%async_computation.5 | async-start | bytes 21626880 | tf_op jit(solution)/shard_map/all_gather | solution.py:11
  248.3 209.1 %reduce-scatter.2.cloned.1.call-start = ((), (), s32[]{:S(2)}) async-start(), calls=%async_computation.3 | async-start | bytes 4718592 | tf_op jit(solution)/shard_map/reduce_scatter | solution.py:64
Sparse Core Ops, SparseCore 0:
  9.2 30.7 all-gather.9
  42.5 140.4 all-gather.7
  208.4 36.1 all-gather.11
  248.4 161.9 all-gather.13
  416.1 34.2 reduce-scatter.1

commit v2 on v0

--- a/solution.py
+++ b/solution.py
@@ -31,7 +31,9 @@
 
 
 def per_device(out_grad, filter_mats, coeffs, pole_rates):
-    full_grad = lax.all_gather(out_grad, "grp", axis=1, tiled=True)
+    full_grad = jnp.concatenate(
+        lax.all_to_all(jnp.stack([out_grad] * lax.axis_size("grp")), "grp", 0, 0), axis=1
+    )
     length = full_grad.shape[0]
     col_width = out_grad.shape[1]
     poles = pole_rates.shape[0]

time: 492 us -> 459 us (0.933)
  waiting for transfers between devices: 236 us -> 195 us
  local copies, waits for them, and re-layouts: 4.96 us -> 12.1 us
    all_gather x1, waiting for transfers between devices: 143 us -> 105 us  [per_device(): lax.all_gather(filter_mats, 'ctx', axis=1, tiled=True)]
    all_gather x1 -> x0, waiting for transfers between devices: 27.7 us -> none  [per_device(): full_grad = lax.all_gather(out_grad, 'grp', axis=1, tiled=True)]
    all_to_all x0 -> x1, waiting for transfers between devices: none -> 24.8 us  [per_device(): lax.all_to_all(jnp.stack([out_grad] * lax.axis_size('grp')), 'grp', 0, 0)]
    reshape x0 -> x2, local copies, waits for them, and re-layouts: none -> 5.4 us  [per_device(): jnp.concatenate(lax.all_to_all(jnp.stack([out_grad] * lax.axis_size('grp'...]
  transfers between devices with their start and end apart: 5 -> 5, of which waited for: 3 -> 3; matrix products, arithmetic and copies ran while one was open for 13% -> 15% of each run, Pallas kernels for 0% -> 0%
where the time goes in v2:
time: 459 us; the launch traced here: 458 us
  waiting for transfers between devices  195 us (42%)
  blocking collectives  148 us (32%)
  matrix products  43.2 us (9%)
  other arithmetic  41.2 us (9%)
  between operations  13.9 us (3%)
  local copies, waits for them, and re-layouts  12.1 us (3%)
    unnamed x1, blocking collectives  148 us
    all_gather x1, waiting for transfers between devices, per_device(): lax.all_gather(filter_mats, 'ctx', axis=1, tiled=True)  105 us
    psum x1, waiting for transfers between devices, per_device(): pole_sum = lax.psum(stacked[length:], 'grp')  63.9 us
    select_n x32, other arithmetic, step(): return jax.tree.map(lambda a, b: jnp.where(reached, a, b), new, before)  39.8 us
    all_to_all x1, waiting for transfers between devices, per_device(): lax.all_to_all(jnp.stack([out_grad] * lax.axis_size('grp')), 'grp', 0, 0)  24.8 us
    dot_general x1, matrix products, per_device(): jnp.einsum('kts,kti->si', kernel_mat, proj_grad, precision=exact_prec)  17.5 us
    dot_general x1, matrix products, per_device(): jnp.einsum('tj,kij->kti', full_grad, lax.all_gather(filter_mats, 'ctx', a...  12.2 us
  transfers between devices with their start and end apart: 5, of which 3 were waited for; matrix products, arithmetic and copies ran while one was open for 15% of the time, Pallas kernels for 0%

profile of v2, /device:TPU:0, one launch (start us, length us, event | category | flops | bytes accessed | tf_op | source)
XLA Modules:
  0.0 457.7 jit_solution(398114570787341983)
XLA Ops:
  7.3 2.4 stack.2
  9.7 3.6 all-to-all-start
  15.5 24.8 %all-to-all-done = bf16[8,512,256]{2,1,0:T(8,128)(2,1)S(1)} async-done(((bf16[8,512,256]{2,1,0:T(8,128)(2,1)}), bf16[8,512,256]{2,1,0:T(8,128)(2,1)S(1)}, u32[]{:S(2)}, u32[]{:S(2)}) %all-to-all-start) | async-done | bytes 2097184 | tf_op jit(solution)/shard_map/all_to_all | solution.py:35
  40.4 2.5 copy.9
  42.9 2.9 reshape.77
  45.8 105.1 %all-gather.4.cloned.1.call-done = bf16[2,2048,2048]{2,1,0:T(8,128)(2,1)} async-done(((bf16[2,64,2048]{2,1,0:T(8,128)(2,1)}), bf16[2,2048,2048]{2,1,0:T(8,128)(2,1)}) %all-gather.4.cloned.1.call-update) | async-done | bytes 16777232 | tf_op jit(solution)/shard_map/all_gather | solution.py:60
  150.9 12.2 %fusion.35 = f32[2,2048,512]{2,1,0:T(8,128)S(1)} fusion(bf16[2,2048,2048]{2,1,0:T(8,128)(2,1)} %all-gather.4.cloned.1.call-done, bf16[512,2048,1]{1,0,2:T(8,128)(2,1)S(1)} %reshape.77), kind=kOutput, calls=%fused_computation.45 | convolution fusion | flops 8589934592 | bytes 27262976 | tf_op jit(solution)/shard_map/tj,kij->kti/dot_general | solution.py:57
  163.1 3.3 copy-done
  166.3 9.1 %fusion.8 = f32[1,80,2048]{2,1,0:T(8,128)} fusion(f32[2,2048,512]{2,1,0:T(8,128)S(1)} %fusion.35, f32[80,512]{1,0:T(8,128)S(1)} %multiply_exponential_fusion, f32[2,80]{1,0:T(2,128)S(1)} %get-tuple-element.167), kind=kOutput, calls=%fused_computation.8 | convolution fusion | flops 2013347840 | bytes 9208448 | tf_op jit(solution)/shard_map/kpt,kti->pi/dot_general | solution.py:64
  175.5 63.9 %all-reduce.3.cloned.1.call-done = f32[1,80,2048]{2,1,0:T(8,128)} async-done(((f32[1,80,2048]{2,1,0:T(8,128)}), f32[1,80,2048]{2,1,0:T(8,128)}) %all-reduce.3.cloned.1.call-update) | async-done | bytes 655376 | tf_op jit(solution)/shard_map/psum | solution.py:67
  239.6 147.6 %all-reduce = f32[2560]{0:T(1024)S(1)} all-reduce(f32[2560]{0:T(1024)S(1)} %get-tuple-element.168), channel_id=2, replica_groups=mesh['ctx'=32,'grp'=8] {'ctx'}, use_global_device_ids=true, to_apply=%add | all-reduce | flops 2560 | bytes 20480
  387.8 1.9 fusion.15
  389.7 17.5 %fusion.5 = f32[512,2048]{1,0:T(8,128)} fusion(f32[2,2048,512]{2,1,0:T(8,128)} %copy-done, f32[2,512,512]{1,2,0:T(8,128)S(1)} %fusion.15, pred[512,512]{0,1:T(8,128)(4,1)S(1)} %iota_compare_fusion), kind=kOutput, calls=%fused_computation.7 | convolution fusion | flops 12885426176 | bytes 14942208 | tf_op jit(solution)/shard_map/kts,kti->si/dot_general | solution.py:63
  407.3 41.4 %while.16 = (s32[]{:T(128)}, f32[80,2048]{1,0:T(8,128)S(1)}, s32[]{:T(128)}, f32[32,80,2048]{2,1,0:T(8,128)}, f32[32,80,1]{1,2,0:T(1,128)S(1)}, /*index=5*/s32[]{:T(128)}, s32[]{:T(128)}, s32[]{:T(128)}, s32[]{:T(128)}) while((s32[]{:T(128)}, f32[80,2048]{1,0:T(8,128)S(1)}, s32[]{:T(128)}, f32[32,80,2048]{2,1,0:T(8,128)}, ...), condition=%wide.region_3.4_spmd.clone, body=%wide.region_2.3_spmd.clone.sunk | while | flops 655368 | bytes 1967215 | solution.py:24
  413.8 1.3 fusion.39
  419.0 1.3 fusion.39
  420.3 1.2 fusion.39
  421.6 1.2 fusion.39
  422.9 1.3 fusion.39
  428.0 1.3 fusion.39
  429.3 1.3 fusion.39
  433.2 1.3 fusion.39
  434.5 1.3 fusion.39
  448.7 2.5 fusion.12
  (85 shorter events, 31.9 us)
Async XLA Ops:
  6.5 6.8 %copy-start.2 = (u32[256]{0:T(256)S(1)}, u32[256]{0:T(256)}, u32[]{:S(2)}) copy-start(u32[256]{0:T(256)} %constant.76) | copy-start | bytes 3076
  6.5 8.1 %copy-start.1 = (f32[80]{0:T(128)S(1)}, f32[80]{0:T(128)}, u32[]{:S(2)}) copy-start(f32[80]{0:T(128)} %param.9) | copy-start | bytes 964
  6.5 144.3 %all-gather.4.cloned.1.call-start = ((), (), s32[]{:S(2)}) async-start(), calls=%async_computation.2 | async-start | bytes 17301504 | tf_op jit(solution)/shard_map/all_gather | solution.py:60
  9.7 30.7 %all-to-all-start = ((bf16[8,512,256]{2,1,0:T(8,128)(2,1)}), bf16[8,512,256]{2,1,0:T(8,128)(2,1)S(1)}, u32[]{:S(2)}, u32[]{:S(2)}) async-start(bf16[8,512,256]{2,1,0:T(8,128)(2,1)} %stack.2), calls=%async_computation | async-start | bytes 4194304 | tf_op jit(solution)/shard_map/all_to_all | solution.py:35
  13.3 226.1 %all-reduce.3.cloned.1.call-start = ((), (), s32[]{:S(2)}) async-start(), calls=%async_computation.4 | async-start | bytes 1310720 | tf_op jit(solution)/shard_map/psum | solution.py:67
  163.1 3.3 copy-start
  175.5 231.8 %all-gather.6.cloned.1.call-start = ((), (), s32[]{:S(2)}) async-start(), calls=%async_computation.5 | async-start | bytes 21626880 | tf_op jit(solution)/shard_map/all_gather | solution.py:11
  239.4 209.3 %reduce-scatter.2.cloned.1.call-start = ((), (), s32[]{:S(2)}) async-start(), calls=%async_computation.3 | async-start | bytes 4718592 | tf_op jit(solution)/shard_map/reduce_scatter | solution.py:66
Sparse Core Ops, SparseCore 0:
  9.9 140.8 all-gather.3
  175.6 63.7 all-reduce.2
  242.0 161.0 all-gather.5
  407.4 35.4 reduce-scatter.1
